TPU v7x, 256 devices: a whole 4x4x8 slice. The times are simulated.
256 devices in a mesh: group: 8 (over x, core), expert: 8 (over z), hid: 4 (over y).
Axes of the slice: x: 4, y: 4, z: 8, core: 2. Of those that a mesh axis runs over, the one named last changes fastest.
Arguments:
- tokens: bfloat16 [2048, 4096], P(('group', 'expert', 'hid')), may hold values from -6 to 6
- expert_ids: int32 [2048, 2], P(('group', 'expert', 'hid')), may hold values from 0 to 7, all different within a row; in each aligned block of 8 rows (0 to 7, 8 to 15, ...) at most 4 rows name the same one
- gate_numer: int32 [2048, 2], P(('group', 'expert', 'hid')), may hold values from 8 to 64
- gate_weight: bfloat16 [8, 4096, 14336], P('group', None, ('expert', 'hid')), may hold values from -0.09375 to 0.09375
- up_weight: bfloat16 [8, 4096, 14336], P('group', None, ('expert', 'hid')), may hold values from -0.09375 to 0.09375
- down_weight: bfloat16 [8, 14336, 4096], P('group', ('expert', 'hid')), may hold values from -0.046875 to 0.046875
Outputs:
- mixed: bfloat16 [2048, 4096], P(('group', 'expert', 'hid'))
Inputs may be any that keep to these rules, and one draw needn't show every extreme that they name: `expert_ids`: A token's 2 ids differ. Within the rows of one device (aligned blocks of 8 rows) no expert is named more than 4 times, and in every draw some block names some expert exactly 4 times.
All inputs are finite; a program needn't handle non-finite values.
Results may differ from a plain program's by a relative error of at most 0.018.
Values may be sent and summed in bfloat16 or wider, within the bound.
No kernel may reach another device: no remote copies, remote signals or barrier semaphores. Data moves between devices by JAX's collectives and lax.ppermute only.
A program may use at most 128 MiB of HBM per device.

v0:
```python
import jax
import jax.numpy as jnp
from jax import lax
from jax.sharding import PartitionSpec as P

TOPK = 2
CAP = 4


def expert_block(block, w_gate, w_up, w_down):
    local = w_gate.shape[0]
    grid = block.reshape(-1, local, CAP, block.shape[-1])
    gate = jnp.einsum("mlcd,ldf->mlcf", grid, w_gate, preferred_element_type=jnp.float32)
    upper = jnp.einsum("mlcd,ldf->mlcf", grid, w_up, preferred_element_type=jnp.float32)
    hidden = (jax.nn.silu(gate) * upper).astype(jnp.bfloat16)
    output = jnp.einsum("mlcf,lfd->mlcd", hidden, w_down, preferred_element_type=jnp.float32)
    return output.reshape(block.shape)


def body(tokens, expert_ids, gate_numer, gate_weight, up_weight, down_weight):
    tok = tokens.shape[0]
    width = tokens.shape[1]
    groups = lax.axis_size("group")
    members = lax.axis_size(("expert", "hid"))
    local = gate_weight.shape[0]
    experts = groups * local
    flat = expert_ids.reshape(tok * TOPK)
    onehot = (flat[:, None] == jnp.arange(experts, dtype=jnp.int32)[None, :]).astype(jnp.int32)
    before = jnp.cumsum(onehot, axis=0) - onehot
    place = jnp.sum(before * onehot, axis=1)
    target = flat * CAP + place
    slot_ids = jnp.arange(experts * CAP, dtype=jnp.int32)
    scatter_mat = (slot_ids[:, None] == target[None, :]).astype(jnp.bfloat16)
    collect_mat = (target[:, None] == slot_ids[None, :]).astype(jnp.bfloat16)
    copies = jnp.repeat(tokens, TOPK, axis=0)
    outgoing = jnp.dot(scatter_mat, copies, preferred_element_type=jnp.float32).astype(jnp.bfloat16)
    outgoing = outgoing.reshape(groups, local * CAP, width)
    arrived = lax.all_to_all(outgoing, "group", split_axis=0, concat_axis=0, tiled=True)
    partial_value = expert_block(
        lax.all_gather(arrived, ("expert", "hid"), axis=0, tiled=True),
        gate_weight,
        up_weight,
        down_weight,
    )
    partial_value = partial_value.reshape(members, groups, local * CAP, width)
    summed = lax.psum_scatter(
        partial_value.astype(jnp.bfloat16), ("expert", "hid"), scatter_dimension=0, tiled=True
    )
    returned = lax.all_to_all(summed, "group", split_axis=1, concat_axis=1, tiled=True)
    results = returned.reshape(experts * CAP, width)
    values = jnp.dot(collect_mat, results, preferred_element_type=jnp.float32)
    route_w = gate_numer.astype(jnp.float32) * (1.0 / 64.0)
    weighted = values.reshape(tok, TOPK, width) * route_w[:, :, None]
    return jnp.sum(weighted, axis=1).astype(jnp.bfloat16)


def solution(mesh):
    return jax.shard_map(
        body,
        mesh=mesh,
        in_specs=(
            P(("group", "expert", "hid"), None),
            P(("group", "expert", "hid"), None),
            P(("group", "expert", "hid"), None),
            P("group", None, ("expert", "hid")),
            P("group", None, ("expert", "hid")),
            P("group", ("expert", "hid"), None),
        ),
        out_specs=P(("group", "expert", "hid"), None),
        check_vma=False,
    )
```

profile of v0, /device:TPU:1, one launch (start us, length us, event | category | flops | bytes accessed | tf_op | source)
XLA Modules:
  0.0 374.8 jit_solution(6712984873349726699)
XLA Ops:
  6.5 0.0 all-gather.2.cloned.1.call-start
  6.5 0.8 copy.27
  7.3 0.1 eq.57
  7.4 0.1 fusion.19
  7.5 0.2 select_reduce_fusion
  7.7 0.9 broadcast_in_dim.2
  8.6 0.1 reshape.74
  8.7 0.2 convolution_convert_fusion
  8.9 0.1 reshape.75
  9.0 12.1 %all_to_all.10 = bf16[8,4,4096]{2,1,0:T(4,128)(2,1)S(1)} all-to-all(bf16[8,4,4096]{2,1,0:T(4,128)(2,1)S(1)} %reshape.75), channel_id=1, replica_groups=mesh['group'=8,'expert'=8,'hid'=4] {'group'}, dimensions={0} | all-to-all | bytes 524288 | tf_op jit(solution)/shard_map/all_to_all | solution.py:38
  21.0 0.9 copy.30
  21.9 0.0 all-gather.2.cloned.1.call-update
  21.9 0.0 all-reduce.3.cloned.1.call-start
  22.0 98.7 %all-gather.2.cloned.1.call-done = bf16[256,4,4096]{2,0,1:T(8,128)(2,1)} async-done(((bf16[8,4,4096]{2,0,1:T(8,128)(2,1)}), bf16[256,4,4096]{2,0,1:T(8,128)(2,1)}) %all-gather.2.cloned.1.call-update) | async-done | bytes 8388624 | tf_op jit(solution)/shard_map/all_gather | solution.py:40
  120.7 7.5 %fusion.3 = f32[256,4,448]{0,2,1:T(8,128)S(1)} fusion(bf16[256,4,4096]{2,0,1:T(8,128)(2,1)} %all-gather.2.cloned.1.call-done, bf16[1,4096,448]{1,2,0:T(8,128)(2,1)} %param.9), kind=kOutput, calls=%fused_computation.6 | convolution fusion | flops 3758096384 | bytes 13893632 | tf_op jit(solution)/shard_map/mlcd,ldf->mlcf/dot_general | solution.py:13
  128.2 15.3 %convert_bitcast_fusion = bf16[32,8,4,4096]{3,1,0,2:T(8,128)(2,1)} fusion(bf16[1,448,4096]{2,1,0:T(8,128)(2,1)} %param.11, bf16[256,4,4096]{2,0,1:T(8,128)(2,1)} %all-gather.2.cloned.1.call-done, bf16[1,4096,448]{1,2,0:T(8,128)(2,1)} %param.10, f32[256,4,448]{0,2,1:T(8,128)S(1)} %fusion.3), kind=kOutput, calls=%fused_computation | convolution fusion | flops 7523139584 | bytes 25952256 | tf_op jit(solution)/shard_map/mlcf,lfd->mlcd/dot_general | solution.py:16
  143.4 0.0 copy-start.1
  143.4 0.0 copy-start
  143.5 0.0 all-reduce.3.cloned.1.call-update
  143.5 0.1 reduce_sum.21
  143.6 0.6 copy-done.1
  144.1 0.6 dynamic-slice
  144.7 208.3 %all-reduce.3.cloned.1.call-done = bf16[32,8,4,4096]{3,1,0,2:T(8,128)(2,1)} async-done(((bf16[32,8,4,4096]{3,1,0,2:T(8,128)(2,1)}), bf16[32,8,4,4096]{3,1,0,2:T(8,128)(2,1)}) %all-reduce.3.cloned.1.call-update) | async-done | bytes 8388624
  353.0 1.6 constant_dynamic-slice_fusion
  354.6 0.9 copy.31
  355.5 5.1 %all-to-all-start.1 = ((bf16[1,8,4,4096]{3,2,0,1:T(4,128)(2,1)}), bf16[1,8,4,4096]{3,2,0,1:T(4,128)(2,1)S(1)}, u32[]{:S(2)}, u32[]{:S(2)}) async-start(bf16[1,8,4,4096]{3,2,0,1:T(4,128)(2,1)} %copy.31), calls=%async_computation.1 | async-start | bytes 524288 | tf_op jit(solution)/shard_map/all_to_all | solution.py:49
  360.6 0.1 copy.29
  360.7 0.0 copy-done
  360.7 6.4 %all-to-all-done.1 = bf16[1,8,4,4096]{3,2,0,1:T(4,128)(2,1)S(1)} async-done(((bf16[1,8,4,4096]{3,2,0,1:T(4,128)(2,1)}), bf16[1,8,4,4096]{3,2,0,1:T(4,128)(2,1)S(1)}, u32[]{:S(2)}, u32[]{:S(2)}) %all-to-all-start.1) | async-done | bytes 262176 | tf_op jit(solution)/shard_map/all_to_all | solution.py:49
  367.1 0.1 reshape.84
  367.1 0.9 fusion.16
  (4 shorter events, 0.1 us)
Async XLA Ops:
  6.5 114.1 %all-gather.2.cloned.1.call-start = ((), (), s32[]{:S(2)}) async-start(), calls=%async_computation.2 | async-start | bytes 8650752 | tf_op jit(solution)/shard_map/all_gather | solution.py:40
  21.9 331.1 %all-reduce.3.cloned.1.call-start = ((), (), s32[]{:S(2)}) async-start(), calls=%async_computation.3 | async-start | bytes 16777216
  143.4 0.7 copy-start.1
  143.4 217.2 %copy-start = (s32[8,2]{0,1:T(2,128)S(1)}, s32[8,2]{0,1:T(2,128)}, u32[]{:S(2)}) copy-start(s32[8,2]{0,1:T(2,128)} %param.8) | copy-start | bytes 196
  355.5 11.6 %all-to-all-start.1 = ((bf16[1,8,4,4096]{3,2,0,1:T(4,128)(2,1)}), bf16[1,8,4,4096]{3,2,0,1:T(4,128)(2,1)S(1)}, u32[]{:S(2)}, u32[]{:S(2)}) async-start(bf16[1,8,4,4096]{3,2,0,1:T(4,128)(2,1)} %copy.31), calls=%async_computation.1 | async-start | bytes 524288 | tf_op jit(solution)/shard_map/all_to_all | solution.py:49
Sparse Core Ops, SparseCore 0:
  22.1 98.5 all-gather.1
  143.6 209.3 all-reduce.2
where the time goes:
time: 375 us
  waiting for transfers between devices  313 us (83%)
  matrix products  23.8 us (6%)
  between operations  13.5 us (4%)
  blocking collectives  12.1 us (3%)
  local copies, waits for them, and re-layouts  6.65 us (2%)
  starting transfers between devices  5.13 us (1%)
    unnamed x3, waiting for transfers between devices  208 us
    all_gather x1, waiting for transfers between devices, body(): lax.all_gather(arrived, ('expert', 'hid'), axis=0, tiled=True)  98.7 us
    dot_general x1, matrix products, expert_block(): jnp.einsum('mlcf,lfd->mlcd', hidden, w_down, preferred_element_type=jnp.f...  15.3 us
    all_to_all x1, blocking collectives, body(): lax.all_to_all(outgoing, 'group', split_axis=0, concat_axis=0, tiled=True)  12.1 us
    dot_general x1, matrix products, expert_block(): jnp.einsum('mlcd,ldf->mlcf', grid, w_gate, preferred_element_type=jnp.flo...  7.52 us
  transfers between devices with their start and end apart: 3, of which 3 were waited for; matrix products, arithmetic and copies ran while one was open for 0% of the time, Pallas kernels for 0%

commit v1 on v0

--- a/solution.py
+++ b/solution.py
@@ -1,3 +1,4 @@
+import functools
 import jax
 import jax.numpy as jnp
 from jax import lax
@@ -5,6 +6,15 @@
 
 TOPK = 2
 CAP = 4
+
+
+def _direct_clusters(xx, link_axis):
+    work_now = tuple((xx for _ in range(jax.lax.axis_size(link_axis))))
+    x_new = jax.lax.all_to_all(jnp.stack(work_now, axis=0), link_axis, 0, 0)
+    return jnp.concatenate(x_new, axis=0)
+
+
+fields_press = functools.partial(_direct_clusters, link_axis=("expert", "hid"))
 
 
 def expert_block(block, w_gate, w_up, w_down):
@@ -36,12 +46,7 @@
     outgoing = jnp.dot(scatter_mat, copies, preferred_element_type=jnp.float32).astype(jnp.bfloat16)
     outgoing = outgoing.reshape(groups, local * CAP, width)
     arrived = lax.all_to_all(outgoing, "group", split_axis=0, concat_axis=0, tiled=True)
-    partial_value = expert_block(
-        lax.all_gather(arrived, ("expert", "hid"), axis=0, tiled=True),
-        gate_weight,
-        up_weight,
-        down_weight,
-    )
+    partial_value = expert_block(fields_press(arrived), gate_weight, up_weight, down_weight)
     partial_value = partial_value.reshape(members, groups, local * CAP, width)
     summed = lax.psum_scatter(
         partial_value.astype(jnp.bfloat16), ("expert", "hid"), scatter_dimension=0, tiled=True

time: 375 us -> 471 us (1.26)
  blocking collectives: 12.1 us -> 207 us
  waiting for transfers between devices: 313 us -> 214 us
    all_to_all x0 -> x1, blocking collectives: none -> 195 us  [_direct_clusters(): x_new = jax.lax.all_to_all(jnp.stack(work_now, axis=0), link_axis, 0, 0)]
    all_gather x1 -> x0, waiting for transfers between devices: 98.7 us -> none  [body(): lax.all_gather(arrived, ('expert', 'hid'), axis=0, tiled=True)]
    unnamed x3 -> x2, waiting for transfers between devices: 208 us -> 208 us
  transfers between devices with their start and end apart: 3 -> 2, of which waited for: 3 -> 2; matrix products, arithmetic and copies ran while one was open for 0% -> 0% of each run, Pallas kernels for 0% -> 0%
where the time goes in v1:
time: 471 us
  waiting for transfers between devices  214 us (45%)
  blocking collectives  207 us (44%)
  matrix products  20.5 us (4%)
  between operations  13.5 us (3%)
  local copies, waits for them, and re-layouts  10.2 us (2%)
  starting transfers between devices  5.09 us (1%)
    unnamed x2, waiting for transfers between devices  208 us
    all_to_all x1, blocking collectives, _direct_clusters(): x_new = jax.lax.all_to_all(jnp.stack(work_now, axis=0), link_axis, 0, 0)  195 us
    dot_general x1, matrix products, expert_block(): jnp.einsum('mlcf,lfd->mlcd', hidden, w_down, preferred_element_type=jnp.f...  15.3 us
    all_to_all x1, blocking collectives, body(): lax.all_to_all(outgoing, 'group', split_axis=0, concat_axis=0, tiled=True)  12.1 us
  transfers between devices with their start and end apart: 2, of which 2 were waited for; matrix products, arithmetic and copies ran while one was open for 0% of the time, Pallas kernels for 0%

profile of v1, /device:TPU:1, one launch (start us, length us, event | category | flops | bytes accessed | tf_op | source)
XLA Modules:
  0.0 470.6 jit_solution(11304576026851386275)
XLA Ops:
  6.5 0.0 all-reduce.3.cloned.1.call-start
  6.5 0.8 copy.29
  7.3 0.1 eq.57
  7.4 0.1 fusion.29
  7.5 0.2 select_reduce_fusion
  7.7 0.9 broadcast_in_dim.2
  8.6 0.1 reshape.77
  8.7 0.2 convolution_convert_fusion
  8.9 0.1 reshape.78
  9.0 12.1 %all_to_all.15 = bf16[8,4,4096]{2,1,0:T(4,128)(2,1)S(1)} all-to-all(bf16[8,4,4096]{2,1,0:T(4,128)(2,1)S(1)} %reshape.78), channel_id=1, replica_groups=mesh['group'=8,'expert'=8,'hid'=4] {'group'}, dimensions={0} | all-to-all | bytes 524288 | tf_op jit(solution)/shard_map/all_to_all | solution.py:48
  21.0 0.1 copy.32
  21.2 1.0 stack.2
  22.2 0.0 copy-start.2
  22.3 194.5 %all_to_all.16 = bf16[32,8,4,4096]{3,1,2,0:T(8,128)(2,1)S(1)} all-to-all(bf16[32,8,4,4096]{3,1,2,0:T(8,128)(2,1)S(1)} %stack.2), channel_id=1, replica_groups=mesh['group'=8,'expert'=8,'hid'=4] {'expert','hid'}, dimensions={0} | all-to-all | bytes 16777216 | tf_op jit(solution)/shard_map/all_to_all | solution.py:13
  216.8 0.0 copy-start
  216.8 3.2 copy-done
  220.0 0.0 copy-done.2
  220.0 4.1 fusion.2
  224.1 15.3 %convert_bitcast_fusion = bf16[32,8,4,4096]{3,1,0,2:T(8,128)(2,1)} fusion(bf16[1,448,4096]{2,1,0:T(8,128)(2,1)} %param.11, bf16[1,4096,448]{1,2,0:T(8,128)(2,1)} %param.10, bf16[32,8,4,4096]{3,1,2,0:T(8,128)(2,1)} %copy-done, f32[256,4,448]{0,2,1:T(8,128)S(1)} %fusion.2), kind=kOutput, calls=%fused_computation.4 | convolution fusion | flops 7523139584 | bytes 25952256 | tf_op jit(solution)/shard_map/mlcf,lfd->mlcd/dot_general | solution.py:26
  239.4 0.0 copy-start.3
  239.4 0.0 copy-start.1
  239.4 0.0 all-reduce.3.cloned.1.call-update
  239.4 0.1 reduce_sum.21
  239.5 0.6 copy-done.3
  240.1 0.6 dynamic-slice
  240.7 208.1 %all-reduce.3.cloned.1.call-done = bf16[32,8,4,4096]{3,1,0,2:T(8,128)(2,1)} async-done(((bf16[32,8,4,4096]{3,1,0,2:T(8,128)(2,1)}), bf16[32,8,4,4096]{3,1,0,2:T(8,128)(2,1)}) %all-reduce.3.cloned.1.call-update) | async-done | bytes 8388624
  448.7 1.6 constant_dynamic-slice_fusion
  450.3 0.9 copy.34
  451.2 5.1 %all-to-all-start.2 = ((bf16[1,8,4,4096]{3,2,0,1:T(4,128)(2,1)}), bf16[1,8,4,4096]{3,2,0,1:T(4,128)(2,1)S(1)}, u32[]{:S(2)}, u32[]{:S(2)}) async-start(bf16[1,8,4,4096]{3,2,0,1:T(4,128)(2,1)} %copy.34), calls=%async_computation.2 | async-start | bytes 524288 | tf_op jit(solution)/shard_map/all_to_all | solution.py:54
  456.3 0.1 copy.31
  456.4 0.0 copy-done.1
  456.4 6.4 %all-to-all-done.2 = bf16[1,8,4,4096]{3,2,0,1:T(4,128)(2,1)S(1)} async-done(((bf16[1,8,4,4096]{3,2,0,1:T(4,128)(2,1)}), bf16[1,8,4,4096]{3,2,0,1:T(4,128)(2,1)S(1)}, u32[]{:S(2)}, u32[]{:S(2)}) %all-to-all-start.2) | async-done | bytes 262176 | tf_op jit(solution)/shard_map/all_to_all | solution.py:54
  462.8 0.1 reshape.88
  462.9 0.9 fusion.26
  (4 shorter events, 0.1 us)
Async XLA Ops:
  6.5 442.2 %all-reduce.3.cloned.1.call-start = ((), (), s32[]{:S(2)}) async-start(), calls=%async_computation.3 | async-start | bytes 16777216
  22.2 197.7 %copy-start.2 = (bf16[1,4096,448]{1,2,0:T(8,128)(2,1)S(1)}, bf16[1,4096,448]{1,2,0:T(8,128)(2,1)}, u32[]{:S(2)}) copy-start(bf16[1,4096,448]{1,2,0:T(8,128)(2,1)} %param.9) | copy-start | bytes 11010052
  216.8 3.2 copy-start
  239.4 0.7 copy-start.3
  239.4 217.0 %copy-start.1 = (s32[8,2]{0,1:T(2,128)S(1)}, s32[8,2]{0,1:T(2,128)}, u32[]{:S(2)}) copy-start(s32[8,2]{0,1:T(2,128)} %param.8) | copy-start | bytes 196
  451.2 11.6 %all-to-all-start.2 = ((bf16[1,8,4,4096]{3,2,0,1:T(4,128)(2,1)}), bf16[1,8,4,4096]{3,2,0,1:T(4,128)(2,1)S(1)}, u32[]{:S(2)}, u32[]{:S(2)}) async-start(bf16[1,8,4,4096]{3,2,0,1:T(4,128)(2,1)} %copy.34), calls=%async_computation.2 | async-start | bytes 524288 | tf_op jit(solution)/shard_map/all_to_all | solution.py:54
Sparse Core Ops, SparseCore 0:
  239.5 209.1 all-reduce.2
